TPU v7x, 768 devices: a whole 4x8x12 slice. The times are simulated.
768 devices in a mesh: row: 16 (over x, y_hi, core), col: 48 (over y_lo, z).
Axes of the slice: x: 4, y: 8 (y_hi: 2, y_lo: 4; y = y_hi * 4 + y_lo), z: 12, core: 2. Of those that a mesh axis runs over, the one named last changes fastest.
Arguments:
- features: bfloat16 [6144, 4096], P('col', 'row'), may hold values from -6 to 6
- weight_blocks: bfloat16 [384, 6, 128, 128], P('col', None, 'row'), may hold values from -0.21875 to 0.21875
- block_rows: int32 [384, 6], P('col'), may hold values from 0 to 47, as said below
- upstream: bfloat16 [49152, 4096], P('col', 'row'), may hold values from -6 to 6
Outputs:
- hidden: bfloat16 [49152, 4096], P('col', 'row')
- input_grad: bfloat16 [6144, 4096], P('col', 'row')
- weight_grad: float32 [384, 6, 128, 128], P('col', None, 'row')
Inputs may be any that keep to these rules, and one draw needn't show every extreme that they name: `block_rows`: the 6 block rows of one block column are distinct.
All inputs are finite; a program needn't handle non-finite values.
Results may differ from a plain program's by a relative error of at most 0.0049.
Values may be sent and summed in bfloat16 or wider, within the bound.
A program may use at most 64 MiB of HBM per device.

v0:
```python
import jax
import jax.numpy as jnp
from jax import lax
from jax.sharding import PartitionSpec as P


def local(features, weight_blocks, block_rows, upstream):
    tok_rows = features.shape[1]
    gathered = lax.all_gather(features, "col", axis=0, tiled=True)
    blocks = gathered.reshape(-1, 128, tok_rows)
    block_count = blocks.shape[0]
    full_weights = lax.all_gather(weight_blocks, "row", axis=2, tiled=True)
    picked = blocks[block_rows]
    preact = jnp.einsum("fskt,fskn->fnt", picked, full_weights, preferred_element_type=jnp.float32)
    hidden = jax.nn.gelu(preact).astype(jnp.bfloat16).reshape(-1, tok_rows)
    _, pullback = jax.vjp(jax.nn.gelu, preact)
    grad_pre = pullback(upstream.reshape(preact.shape).astype(jnp.float32))[0].astype(jnp.bfloat16)
    input_part = jnp.einsum(
        "fnt,fskn->fskt", grad_pre, full_weights, preferred_element_type=jnp.float32
    )
    flat_part = input_part.reshape(-1, 128, tok_rows)
    flat_rows = block_rows.reshape(-1)
    grad_scale = float(tok_rows * lax.axis_size("row")) ** (-0.5)
    weight_terms = jnp.einsum(
        "fskt,fnt->fskn", picked, grad_pre, preferred_element_type=jnp.float32
    )
    weight_grad = (
        lax.psum_scatter(weight_terms, "row", scatter_dimension=2, tiled=True) * grad_scale
    )
    input_terms = (
        jnp.zeros((block_count, 128, tok_rows), jnp.float32)
        .at[flat_rows]
        .add(flat_part)
        .reshape(-1, tok_rows)
    )
    summed = lax.psum_scatter(input_terms, "col", scatter_dimension=0, tiled=True)
    return (hidden, summed.astype(jnp.bfloat16), weight_grad)


def solution(mesh):
    return jax.shard_map(
        local,
        mesh=mesh,
        in_specs=(P("col", "row"), P("col", None, "row", None), P("col", None), P("col", "row")),
        out_specs=(P("col", "row"), P("col", "row"), P("col", None, "row", None)),
        check_vma=False,
    )
```

profile of v0, /device:TPU:6, one launch (start us, length us, event | category | flops | bytes accessed | tf_op | source)
XLA Modules:
  0.0 686.2 jit_solution(10085543042145102361)
XLA Ops:
  7.2 0.0 all-gather.3.cloned.1.call-start
  7.2 0.7 all-gather.3.cloned.1.call-update
  7.9 0.0 all-gather.5.cloned.1.call-start
  7.9 0.7 all-gather.5.cloned.1.call-update
  8.6 0.0 reduce-scatter.5.cloned.1.call-start
  8.7 0.7 compare_select_fusion
  9.4 0.1 reshape.60
  9.5 238.1 %all-gather.3.cloned.1.call-done = bf16[6144,256]{1,0:T(8,128)(2,1)} async-done(((bf16[128,256]{1,0:T(8,128)(2,1)}), bf16[6144,256]{1,0:T(8,128)(2,1)}) %all-gather.3.cloned.1.call-update) | async-done | bytes 3145744 | tf_op jit(solution)/shard_map/all_gather | solution.py:9
  247.6 2.6 gather_fusion
  250.2 60.7 %all-gather.5.cloned.1.call-done = bf16[8,6,128,128]{3,2,1,0:T(8,128)(2,1)} async-done(((bf16[8,6,8,128]{3,2,1,0:T(8,128)(2,1)}), bf16[8,6,128,128]{3,2,1,0:T(8,128)(2,1)}) %all-gather.5.cloned.1.call-update) | async-done | bytes 1572880 | tf_op jit(solution)/shard_map/all_gather | solution.py:12
  310.9 0.0 copy-start.3
  310.9 3.0 multiply_convert_fusion
  314.0 0.0 copy-start.1
  314.0 1.0 copy-done.1
  315.0 0.0 copy-done.3
  315.0 2.8 fusion.10
  317.7 0.0 reduce-scatter.5.cloned.1.call-update
  317.8 0.0 reduce-scatter.3.cloned.1.call-start
  317.8 0.0 copy-done.5
  317.8 0.1 reshape.54
  317.9 1.2 copy-done
  319.2 0.3 copy-done.2
  319.4 0.1 copy-done.4
  319.6 4.0 fusion.12
  323.5 6.6 copy.9
  330.1 3.4 broadcast_in_dim.8
  333.5 15.5 %scatter_fusion = f32[48,128,256]{2,1,0:T(8,128)} fusion(f32[48,128,256]{2,1,0:T(8,128)} %broadcast_in_dim.8, s32[48]{0:T(128)S(1)} %fusion.14, f32[48,128,256]{2,1,0:T(8,128)} %copy.9), kind=kCustom, calls=%fused_computation.1 | custom fusion | flops 1572864 | bytes 18874560 | tf_op jit(solution)/shard_map/scatter-add | solution.py:33
  349.0 0.0 reduce-scatter.3.cloned.1.call-update
  349.1 77.1 %reduce-scatter.5.cloned.1.call-done = f32[8,6,8,128]{3,2,1,0:T(8,128)} async-done(((f32[8,6,128,128]{3,2,1,0:T(8,128)}), f32[8,6,8,128]{3,2,1,0:T(8,128)}) %reduce-scatter.5.cloned.1.call-update) | async-done | bytes 196624 | tf_op jit(solution)/shard_map/reduce_scatter | solution.py:28
  426.1 1.6 broadcast_multiply_fusion
  427.7 250.4 %reduce-scatter.3.cloned.1.call-done = f32[128,256]{1,0:T(8,128)} async-done(((f32[6144,256]{1,0:T(8,128)}), f32[128,256]{1,0:T(8,128)}) %reduce-scatter.3.cloned.1.call-update) | async-done | bytes 131088 | tf_op jit(solution)/shard_map/reduce_scatter | solution.py:36
  678.1 1.5 convert_element_type.19
  (6 shorter events, 0.0 us)
Async XLA Ops:
  7.2 240.4 %all-gather.3.cloned.1.call-start = ((), (), s32[]{:S(2)}) async-start(), calls=%async_computation.2 | async-start | bytes 3211264 | tf_op jit(solution)/shard_map/all_gather | solution.py:9
  7.9 303.0 %all-gather.5.cloned.1.call-start = ((), (), s32[]{:S(2)}) async-start(), calls=%async_computation.3 | async-start | bytes 1671168 | tf_op jit(solution)/shard_map/all_gather | solution.py:12
  8.6 417.5 %reduce-scatter.5.cloned.1.call-start = ((), (), s32[]{:S(2)}) async-start(), calls=%async_computation.5 | async-start | bytes 3342336 | tf_op jit(solution)/shard_map/reduce_scatter | solution.py:28
  310.9 4.0 copy-start.3
  314.0 1.0 copy-start.1
  315.0 2.9 copy-start.5
  317.7 1.4 copy-start
  317.7 1.7 copy-start.2
  317.7 1.8 copy-start.4
  317.8 360.3 %reduce-scatter.3.cloned.1.call-start = ((), (), s32[]{:S(2)}) async-start(), calls=%async_computation.4 | async-start | bytes 6422528 | tf_op jit(solution)/shard_map/reduce_scatter | solution.py:36
Sparse Core Ops, SparseCore 0:
  10.4 237.1 all-gather.2
  251.3 59.6 all-gather.4
  317.9 108.1 reduce-scatter.4
  429.1 248.9 reduce-scatter.2
where the time goes:
time: 687 us; the launch traced here: 686 us
  waiting for transfers between devices  628 us (91%)
  other arithmetic  19.3 us (3%)
  local copies, waits for them, and re-layouts  15.4 us (2%)
  between operations  13.8 us (2%)
  matrix products  9.8 us (1%)
    reduce_scatter x1, waiting for transfers between devices, local(): lax.psum_scatter(input_terms, 'col', scatter_dimension=0, tiled=True)  250 us
    all_gather x1, waiting for transfers between devices, local(): gathered = lax.all_gather(features, 'col', axis=0, tiled=True)  238 us
    reduce_scatter x1, waiting for transfers between devices, local(): lax.psum_scatter(weight_terms, 'row', scatter_dimension=2, tiled=True)  77.1 us
    all_gather x1, waiting for transfers between devices, local(): full_weights = lax.all_gather(weight_blocks, 'row', axis=2, tiled=True)  60.7 us
    scatter-add x1, other arithmetic, local(): input_terms = jnp.zeros((block_count, 128, tok_rows), jnp.float32).at[fla...  15.5 us
  transfers between devices with their start and end apart: 4, of which 4 were waited for; matrix products, arithmetic and copies ran while one was open for 5% of the time, Pallas kernels for 0%

commit v1 on v0

v1 whole, which is shorter than its diff:
```python
import functools
import math

import jax
import jax.numpy as jnp
from jax import lax
from jax.experimental import pallas as pl
from jax.experimental.pallas import tpu as pltpu
from jax.sharding import PartitionSpec as P

Y, Z = 4, 12
X = 4
HALF_RING = Z // 2
PLUS, MINUS = 0, 1
VMEM = pltpu.VMEM


def places():
    col = lax.axis_index("col")
    row = lax.axis_index("row")
    y, z = col // Z, col % Z
    x, h, core = row // 4, (row // 2) % 2, row % 2

    def col_of(dy, dz):
        return ((y + dy + Y) % Y) * Z + (z + dz + Z) % Z

    def row_of(dx, dh, dc):
        return (((x + dx + X) % X) * 2 + (h + dh) % 2) * 2 + (core + dc) % 2

    return col_of, row_of


def enter(col_of, row_of):
    barrier = pltpu.get_barrier_semaphore()
    cols = [col_of(1, 0), col_of(2, 0), col_of(3, 0), col_of(0, 1), col_of(0, -1)]
    rows = [row_of(0, 0, 1), row_of(0, 1, 0), row_of(1, 0, 0), row_of(-1, 0, 0)]
    for c in cols:
        pl.semaphore_signal(barrier, inc=1, device_id={"col": c})
    for r in rows:
        pl.semaphore_signal(barrier, inc=1, device_id={"row": r})
    pl.semaphore_wait(barrier, len(cols) + len(rows))


def gather_kernel(feat, wts, feat_all, wts_all, ys, yr, zs, zr, ws, wr):
    col_of, row_of = places()
    me_col, me_row = col_of(0, 0), row_of(0, 0, 0)
    half = feat.shape[0] // 2
    started = []

    def send(src, dst, send_sem, recv_sem, **to):
        copy = pltpu.make_async_remote_copy(
            src_ref=src, dst_ref=dst, send_sem=send_sem, recv_sem=recv_sem, device_id=to
        )
        copy.start()
        started.append(copy)
        return copy

    def send_w(i, slot, src, to):
        return send(src, wts_all.at[slot], ws.at[i], wr.at[i], row=to)

    def send_z(way, k, j):
        step = 1 if way == PLUS else -1
        slot = col_of(j, -step * (k - 1))
        src = feat if (j == 0 and k == 1) else feat_all.at[slot]
        dst = feat_all.at[slot]
        if k == HALF_RING:
            part = pl.ds(0, half) if way == PLUS else pl.ds(half, half)
            src, dst = src.at[part], dst.at[part]
        return send(src, dst, zs.at[way, k - 1, j], zr.at[way, k - 1, j], col=col_of(0, step))

    enter(col_of, row_of)
    core_to, h_to = row_of(0, 0, 1), row_of(0, 1, 0)
    x_up, x_down = row_of(1, 0, 0), row_of(-1, 0, 0)

    zc = {}
    yc = {}
    for way in (PLUS, MINUS):
        zc[way, 1, 0] = send_z(way, 1, 0)
    for j in (1, 3, 2):
        yc[j] = send(feat, feat_all.at[me_col], ys.at[j - 1], yr.at[j - 1], col=col_of(4 - j, 0))
    w_h = send_w(0, me_row, wts, h_to)
    w_up = send_w(1, me_row, wts, x_up)
    w_down = send_w(2, me_row, wts, x_down)
    cores = [send_w(7, me_row, wts, core_to)]
    feat_all[me_col] = feat[...]
    wts_all[me_row] = wts[...]

    def w_stage_x():
        w_up.wait_recv()
        slot = row_of(-1, 0, 0)
        first = send_w(3, slot, wts_all.at[slot], x_up)
        cores.append(send_w(8, slot, wts_all.at[slot], core_to))
        w_down.wait_recv()
        slot = row_of(1, 0, 0)
        cores.append(send_w(9, slot, wts_all.at[slot], core_to))
        w_h.wait_recv()
        slot = row_of(0, 1, 0)
        up = send_w(4, slot, wts_all.at[slot], x_up)
        down = send_w(5, slot, wts_all.at[slot], x_down)
        cores.append(send_w(10, slot, wts_all.at[slot], core_to))
        return first, up, down

    def w_stage_far(first, up, down):
        down.wait_recv()
        slot = row_of(1, 1, 0)
        last = send_w(6, slot, wts_all.at[slot], x_down)
        cores.append(send_w(11, slot, wts_all.at[slot], core_to))
        up.wait_recv()
        slot = row_of(-1, 1, 0)
        cores.append(send_w(12, slot, wts_all.at[slot], core_to))
        first.wait_recv()
        slot = row_of(2, 0, 0)
        cores.append(send_w(13, slot, wts_all.at[slot], core_to))
        return last

    def w_stage_last(last):
        last.wait_recv()
        slot = row_of(2, 1, 0)
        cores.append(send_w(14, slot, wts_all.at[slot], core_to))

    for j in (1, 3, 2):
        yc[j].wait_recv()
        for way in (PLUS, MINUS):
            zc[way, 1, j] = send_z(way, 1, j)
    pending = None
    for k in range(2, HALF_RING + 1):
        for j in (0, 1, 3, 2):
            for way in (PLUS, MINUS):
                zc[way, k - 1, j].wait_recv()
                zc[way, k, j] = send_z(way, k, j)
        if k == 2:
            pending = w_stage_x()
        elif k == 3:
            pending = w_stage_far(*pending)
        elif k == 4:
            w_stage_last(pending)
    for copy in cores:
        copy.wait_recv()
    for j in range(Y):
        for way in (PLUS, MINUS):
            zc[way, HALF_RING, j].wait_recv()
    for copy in started:
        copy.wait_send()


def gather(features, weights):
    dma = pltpu.SemaphoreType.DMA
    return pl.pallas_call(
        gather_kernel,
        out_shape=(
            jax.ShapeDtypeStruct((Y * Z,) + features.shape, features.dtype),
            jax.ShapeDtypeStruct((X * 4,) + weights.shape, weights.dtype),
        ),
        in_specs=[pl.BlockSpec(memory_space=VMEM)] * 2,
        out_specs=(pl.BlockSpec(memory_space=VMEM),) * 2,
        scratch_shapes=[
            dma((Y - 1,)), dma((Y - 1,)),
            dma((2, HALF_RING, Y)), dma((2, HALF_RING, Y)),
            dma((15,)), dma((15,)),
        ],
        compiler_params=pltpu.CompilerParams(collective_id=1, has_side_effects=True),
        name="gather_features_weights",
    )(features, weights)


def compute_kernel(rows, blocks, wts, upper, hidden, in_part, w_part):
    in_part[...] = jnp.zeros_like(in_part)
    c = math.sqrt(2.0 / math.pi)
    cols, slots = wts.shape[0], wts.shape[1]
    n_owner = w_part.shape[0]
    for f in range(cols):
        at = [rows[f, s] for s in range(slots)]
        picked = jnp.concatenate([blocks[a] for a in at], axis=0)
        w = wts[f].reshape(slots * 128, 128)
        v = lax.dot_general(w, picked, (((0,), (0,)), ((), ())), preferred_element_type=jnp.float32)
        sq = v * v
        t = jnp.tanh(c * (v + 0.044715 * (sq * v)))
        gate = 0.5 * (1.0 + t)
        here = pl.ds(f * 128, 128)
        hidden[here, :] = (v * gate).astype(jnp.bfloat16)
        slope = gate + 0.5 * v * (1.0 - t * t) * (c * (1.0 + (3 * 0.044715) * sq))
        g = (upper[here, :].astype(jnp.float32) * slope).astype(jnp.bfloat16)
        part = jnp.dot(w, g, preferred_element_type=jnp.float32)
        for s in range(slots):
            in_part[at[s]] += part[s * 128 : (s + 1) * 128]
        wg = lax.dot_general(picked, g, (((1,), (1,)), ((), ())), preferred_element_type=jnp.float32)
        for s in range(slots):
            w_part[:, pl.ds((f * slots + s) * 8, 8), :] = wg[s * 128 : (s + 1) * 128].reshape(
                n_owner, 8, 128
            )


def compute(rows, blocks, wts, upper):
    f, s = rows.shape
    return pl.pallas_call(
        compute_kernel,
        out_shape=(
            jax.ShapeDtypeStruct(upper.shape, jnp.bfloat16),
            jax.ShapeDtypeStruct(blocks.shape, jnp.float32),
            jax.ShapeDtypeStruct((X * 4, f * s * 8, 128), jnp.float32),
        ),
        in_specs=[pl.BlockSpec(memory_space=pltpu.SMEM)] + [pl.BlockSpec(memory_space=VMEM)] * 3,
        out_specs=(pl.BlockSpec(memory_space=VMEM),) * 3,
        name="block_columns",
    )(rows, blocks, wts, upper)


def reduce_kernel(
    scale, in_part, w_part, in_out, w_out,
    zbuf_s, zbuf_r, ybuf_s, ybuf_r, cbuf_s, cbuf_r, own, xbuf_s, xbuf_r,
    zs, zr, ys, yr, cs, cr, xs, xr,
):
    col_of, row_of = places()
    half = in_part.shape[1] // 2
    f32, bf16 = jnp.float32, jnp.bfloat16
    started = []
    order = (2, 1, 3, 0)

    def send(src, dst, send_sem, recv_sem, **to):
        copy = pltpu.make_async_remote_copy(
            src_ref=src, dst_ref=dst, send_sem=send_sem, recv_sem=recv_sem, device_id=to
        )
        copy.start()
        started.append(copy)
        return copy

    def send_z(way, k, j):
        step = 1 if way == PLUS else -1
        src, dst = zbuf_s.at[way, k, j], zbuf_r.at[way, k, j]
        if k == 0:
            part = pl.ds(0, half) if way == PLUS else pl.ds(half, half)
            src, dst = src.at[part], dst.at[part]
        return send(src, dst, zs.at[way, k, j], zr.at[way, k, j], col=col_of(0, step))

    def send_x(i, to):
        return send(xbuf_s.at[i], xbuf_r.at[i], xs.at[i], xr.at[i], row=to)

    enter(col_of, row_of)
    core_to, h_to = row_of(0, 0, 1), row_of(0, 1, 0)
    x_up, x_down = row_of(1, 0, 0), row_of(-1, 0, 0)

    zc = {}
    for j in order:
        far = col_of(j, HALF_RING)
        for way in (PLUS, MINUS):
            part = pl.ds(0, half) if way == PLUS else pl.ds(half, half)
            zbuf_s[way, 0, j, part, :] = in_part[far, part, :].astype(bf16)
            zc[way, 0, j] = send_z(way, 0, j)

    dests = [(2, 0), (2, 1), (1, 0), (1, 1), (-1, 0), (-1, 1), (0, 1), (0, 0)]
    cc = []
    for i, (dx, dh) in enumerate(dests):
        cbuf_s[i] = w_part[row_of(dx, dh, 1)].astype(bf16)
        cc.append(send(cbuf_s.at[i], cbuf_r.at[i], cs.at[i], cr.at[i], row=core_to))

    def pair(i):
        dx, dh = dests[i]
        cc[i].wait_recv()
        return w_part[row_of(dx, dh, 0)] + cbuf_r[i].astype(f32)

    xc = {}

    def w_far():
        xbuf_s[0] = pair(0).astype(bf16)
        xc[0] = send_x(0, x_up)
        xbuf_s[1] = pair(1).astype(bf16)
        xc[1] = send_x(1, x_down)
        xbuf_s[2] = pair(3).astype(bf16)
        xc[2] = send_x(2, x_up)
        xbuf_s[3] = pair(4).astype(bf16)
        xc[3] = send_x(3, x_down)

    def w_near():
        xc[0].wait_recv()
        xbuf_s[4] = (pair(2) + xbuf_r[0].astype(f32)).astype(bf16)
        xc[4] = send_x(4, x_up)
        xc[1].wait_recv()
        xbuf_s[5] = (pair(5) + xbuf_r[1].astype(f32)).astype(bf16)
        xc[5] = send_x(5, x_down)
        own[...] = pair(7)

    def w_across():
        xc[2].wait_recv()
        xc[5].wait_recv()
        total = pair(6) + xbuf_r[2].astype(f32) + xbuf_r[5].astype(f32)
        xbuf_s[6] = total.astype(bf16)
        xc[6] = send_x(6, h_to)

    def w_end():
        xc[3].wait_recv()
        xc[4].wait_recv()
        xc[6].wait_recv()
        total = own[...] + xbuf_r[3].astype(f32) + xbuf_r[4].astype(f32) + xbuf_r[6].astype(f32)
        w_out[...] = total * scale

    def add_z(way, k, j):
        step = 1 if way == PLUS else -1
        slot = col_of(j, step * (HALF_RING - k))
        zc[way, k - 1, j].wait_recv()
        if k > 1:
            zbuf_s[way, k, j] = (in_part[slot] + zbuf_r[way, k - 1, j].astype(f32)).astype(bf16)
            return
        got = pl.ds(0, half) if way == PLUS else pl.ds(half, half)
        rest = pl.ds(half, half) if way == PLUS else pl.ds(0, half)
        zbuf_s[way, k, j, got, :] = (
            in_part[slot, got, :] + zbuf_r[way, 0, j, got, :].astype(f32)
        ).astype(bf16)
        zbuf_s[way, k, j, rest, :] = in_part[slot, rest, :].astype(bf16)

    stages = {1: w_far, 2: w_near, 3: w_across, 4: w_end}
    for k in range(1, HALF_RING):
        for j in order:
            for way in (PLUS, MINUS):
                add_z(way, k, j)
                zc[way, k, j] = send_z(way, k, j)
        if k in stages:
            stages[k]()

    def total_z(j):
        for way in (PLUS, MINUS):
            zc[way, HALF_RING - 1, j].wait_recv()
        return (
            in_part[col_of(j, 0)]
            + zbuf_r[PLUS, HALF_RING - 1, j].astype(f32)
            + zbuf_r[MINUS, HALF_RING - 1, j].astype(f32)
        )

    yc = []
    for j in (2, 1, 3):
        ybuf_s[j - 1] = total_z(j).astype(bf16)
        yc.append(
            send(ybuf_s.at[j - 1], ybuf_r.at[j - 1], ys.at[j - 1], yr.at[j - 1], col=col_of(j, 0))
        )
    total = total_z(0)
    for copy in yc:
        copy.wait_recv()
    for j in range(Y - 1):
        total = total + ybuf_r[j].astype(f32)
    in_out[...] = total.astype(bf16)
    for copy in started:
        copy.wait_send()


def reduce(in_part, w_part, scale):
    dma = pltpu.SemaphoreType.DMA
    block, piece = in_part.shape[1:], w_part.shape[1:]
    bf16 = jnp.bfloat16
    return pl.pallas_call(
        functools.partial(reduce_kernel, scale),
        out_shape=(
            jax.ShapeDtypeStruct(block, bf16),
            jax.ShapeDtypeStruct(piece, jnp.float32),
        ),
        in_specs=[pl.BlockSpec(memory_space=VMEM)] * 2,
        out_specs=(pl.BlockSpec(memory_space=VMEM),) * 2,
        scratch_shapes=[
            VMEM((2, HALF_RING, Y) + block, bf16), VMEM((2, HALF_RING, Y) + block, bf16),
            VMEM((Y - 1,) + block, bf16), VMEM((Y - 1,) + block, bf16),
            VMEM((8,) + piece, bf16), VMEM((8,) + piece, bf16),
            VMEM(piece, jnp.float32),
            VMEM((7,) + piece, bf16), VMEM((7,) + piece, bf16),
            dma((2, HALF_RING, Y)), dma((2, HALF_RING, Y)),
            dma((Y - 1,)), dma((Y - 1,)),
            dma((8,)), dma((8,)),
            dma((7,)), dma((7,)),
        ],
        compiler_params=pltpu.CompilerParams(collective_id=2, has_side_effects=True),
        name="reduce_gradients",
    )(in_part, w_part)


def local(features, weight_blocks, block_rows, upstream):
    cols, slots, rows_here, n = weight_blocks.shape
    grad_scale = float(features.shape[1] * lax.axis_size("row")) ** (-0.5)
    blocks, pieces = gather(features, weight_blocks.reshape(-1, n))
    weights = (
        pieces.reshape(-1, cols, slots, rows_here, n)
        .transpose(1, 2, 0, 3, 4)
        .reshape(cols, slots, -1, n)
    )
    hidden, in_part, w_part = compute(block_rows, blocks, weights, upstream)
    input_grad, w_grad = reduce(in_part, w_part, grad_scale)
    return (hidden, input_grad, w_grad.reshape(weight_blocks.shape))


def solution(mesh):
    return jax.shard_map(
        local,
        mesh=mesh,
        in_specs=(P("col", "row"), P("col", None, "row", None), P("col", None), P("col", "row")),
        out_specs=(P("col", "row"), P("col", "row"), P("col", None, "row", None)),
        check_vma=False,
    )
```

time: 687 us -> 124 us (0.18)
  waiting for transfers between devices: 628 us -> 0 us
  Pallas kernels: 0 us -> 116 us
  other arithmetic: 19.3 us -> 0 us
  between operations: 13.8 us -> 0.65 us
  matrix products: 9.8 us -> 0 us
  local copies, waits for them, and re-layouts: 15.4 us -> 6.15 us
    reduce_scatter x2 -> x0, waiting for transfers between devices: 327 us -> none  [the longest x1 250 us: local(): lax.psum_scatter(input_terms, 'col', scatter_dimension=0, tiled=True)]
    all_gather x2 -> x0, waiting for transfers between devices: 299 us -> none  [the longest x1 238 us: local(): gathered = lax.all_gather(features, 'col', axis=0, tiled=True)]
    pallas_call x0 -> x3, Pallas kernels: none -> 116 us  [the longest x1 62.4 us: gather(): pl.pallas_call(gather_kernel, out_shape=(jax.ShapeDtypeStruct((Y * Z,) +...]
    scatter-add x1 -> x0, other arithmetic: 15.5 us -> none  [local(): input_terms = jnp.zeros((block_count, 128, tok_rows), jnp.float32).at[fla...]
    dot_general x3 -> x0, matrix products: 9.8 us -> none  [the longest x1 3.97 us: local(): jnp.einsum('fnt,fskn->fskt', grad_pre, full_weights, preferred_element_ty...]
  transfers between devices with their start and end apart: 4 -> 0, of which waited for: 4 -> 0; matrix products, arithmetic and copies ran while one was open for 5% -> 0% of each run, Pallas kernels for 0% -> 0%
where the time goes in v1:
time: 124 us; the launch traced here: 123 us
  Pallas kernels  116 us (94%)
  local copies, waits for them, and re-layouts  6.15 us (5%)
    pallas_call x1, Pallas kernels, gather(): pl.pallas_call(gather_kernel, out_shape=(jax.ShapeDtypeStruct((Y * Z,) +...  62.4 us
    pallas_call x1, Pallas kernels, reduce(): pl.pallas_call(functools.partial(reduce_kernel, scale), out_shape=(jax.Sh...  43 us
    pallas_call x1, Pallas kernels, compute(): pl.pallas_call(compute_kernel, out_shape=(jax.ShapeDtypeStruct(upper.shap...  10.8 us
    unnamed x2, local copies, waits for them, and re-layouts  3.09 us
    reshape x1, local copies, waits for them, and re-layouts, local(): pieces.reshape(-1, cols, slots, rows_here, n).transpose(1, 2, 0, 3, 4)  3.06 us

profile of v1, /device:TPU:6, one launch (start us, length us, event | category | flops | bytes accessed | tf_op | source)
XLA Modules:
  0.0 123.0 jit_solution(499716352621212361)
XLA Ops:
  0.6 62.4 %gather_features_weights.1 = (bf16[48,128,256]{2,1,0:T(8,128)(2,1)}, bf16[16,384,128]{2,1,0:T(8,128)(2,1)}) custom-call(bf16[128,256]{1,0:T(8,128)(2,1)} %feat.1, bf16[384,128]{1,0:T(8,128)(2,1)} %bitcast.11), custom_call_target="tpu_custom_call" | custom-call | tf_op jit(solution)/shard_map/gather_features_weights/pallas_call | solution.py:148
  63.0 3.1 %copy.9 = bf16[16,8,6,8,128]{4,3,0,2,1:T(8,128)(2,1)} copy(bf16[16,8,6,8,128]{4,3,2,1,0:T(8,128)(2,1)} %bitcast.9) | data formatting | bytes 3145728 | tf_op jit(solution)/shard_map/reshape | solution.py:377
  66.1 10.8 %block_columns.1 = (bf16[1024,256]{1,0:T(8,128)(2,1)}, f32[48,128,256]{2,1,0:T(8,128)}, f32[16,384,128]{2,1,0:T(8,128)}) custom-call(s32[8,6]{1,0:T(8,128)} %rows.1, bf16[48,128,256]{2,1,0:T(8,128)(2,1)} %get-tuple-element.10.blocks, bf16[8,6,128,128]{3,2,1,0:T(8,128)(2,1)} %bitcast.8, bf16[1024,256]{1,0:T(8,128)(2,1)} %upper.1), custom_call_target="tpu_custom_call" | custom-call | tf_op jit(solution)/shard_map/block_columns/pallas_call | solution.py:195
  76.9 43.0 %reduce_gradients.1 = (bf16[128,256]{1,0:T(8,128)(2,1)}, f32[384,128]{1,0:T(8,128)}) custom-call(f32[48,128,256]{2,1,0:T(8,128)} %get-tuple-element.13.in_part, f32[16,384,128]{2,1,0:T(8,128)} %get-tuple-element.14.w_part), custom_call_target="tpu_custom_call" | custom-call | tf_op jit(solution)/shard_map/reduce_gradients/pallas_call | solution.py:348
  119.9 1.5 %copy.12 = bf16[128,256]{1,0:T(8,128)(2,1)} copy(bf16[128,256]{1,0:T(8,128)(2,1)} %get-tuple-element.21) | data formatting | bytes 131072
  121.4 1.6 %copy.13 = f32[8,6,8,128]{3,2,1,0:T(8,128)} copy(f32[8,6,8,128]{3,2,1,0:T(8,128)} %bitcast.10) | data formatting | bytes 393216

commit v2 on v1

v2 whole, which is shorter than its diff:
```python
import functools
import math

import jax
import jax.numpy as jnp
from jax import lax
from jax.experimental import pallas as pl
from jax.experimental.pallas import tpu as pltpu
from jax.sharding import PartitionSpec as P

Y, Z = 4, 12
X = 4
HALF_RING = Z // 2
PLUS, MINUS = 0, 1
VMEM = pltpu.VMEM


def places():
    col = lax.axis_index("col")
    row = lax.axis_index("row")
    y, z = col // Z, col % Z
    x, h, core = row // 4, (row // 2) % 2, row % 2

    def col_of(dy, dz):
        return ((y + dy + Y) % Y) * Z + (z + dz + Z) % Z

    def row_of(dx, dh, dc):
        return (((x + dx + X) % X) * 2 + (h + dh) % 2) * 2 + (core + dc) % 2

    return col_of, row_of


def enter(col_of, row_of):
    barrier = pltpu.get_barrier_semaphore()
    cols = [col_of(1, 0), col_of(2, 0), col_of(3, 0), col_of(0, 1), col_of(0, -1)]
    rows = [row_of(0, 0, 1), row_of(0, 1, 0), row_of(1, 0, 0), row_of(-1, 0, 0)]
    for c in cols:
        pl.semaphore_signal(barrier, inc=1, device_id={"col": c})
    for r in rows:
        pl.semaphore_signal(barrier, inc=1, device_id={"row": r})
    pl.semaphore_wait(barrier, len(cols) + len(rows))


def step_kernel(
    scale, rows, feat, wts, upper, hidden, in_out, w_out,
    feat_all, wts_all, places_of, grad, term, w_part,
    zbuf_s, zbuf_r, ybuf_s, ybuf_r, cbuf_s, cbuf_r, own, xbuf_s, xbuf_r,
    gys, gyr, gzs, gzr, gws, gwr, local_sem,
    zs, zr, ys, yr, cs, cr, xs, xr,
):
    col_of, row_of = places()
    me_col, me_row = col_of(0, 0), row_of(0, 0, 0)
    half = feat.shape[0] // 2
    f32, bf16 = jnp.float32, jnp.bfloat16
    columns, slots = rows.shape
    no_block = columns * slots
    started = []

    def send(src, dst, send_sem, recv_sem, **to):
        copy = pltpu.make_async_remote_copy(
            src_ref=src, dst_ref=dst, send_sem=send_sem, recv_sem=recv_sem, device_id=to
        )
        copy.start()
        started.append(copy)
        return copy

    def w_at(slot):
        return wts_all.at[pl.ds(0, no_block), pl.ds(pl.multiple_of(slot * 8, 8), 8), :]

    def gather_w(i, slot, to, src=None):
        return send(w_at(slot) if src is None else src, w_at(slot), gws.at[i], gwr.at[i], row=to)

    def gather_z(way, k, j):
        step = 1 if way == PLUS else -1
        slot = col_of(j, -step * (k - 1))
        src = feat if (j == 0 and k == 1) else feat_all.at[slot]
        dst = feat_all.at[slot]
        if k == HALF_RING:
            part = pl.ds(0, half) if way == PLUS else pl.ds(half, half)
            src, dst = src.at[part], dst.at[part]
        return send(src, dst, gzs.at[way, k - 1, j], gzr.at[way, k - 1, j], col=col_of(0, step))

    enter(col_of, row_of)
    core_to, h_to = row_of(0, 0, 1), row_of(0, 1, 0)
    x_up, x_down = row_of(1, 0, 0), row_of(-1, 0, 0)

    zc = {}
    yc = {}
    for way in (PLUS, MINUS):
        zc[way, 1, 0] = gather_z(way, 1, 0)
    for j in (1, 3, 2):
        yc[j] = send(feat, feat_all.at[me_col], gys.at[j - 1], gyr.at[j - 1], col=col_of(4 - j, 0))
    w_h = gather_w(0, me_row, h_to, wts)
    w_up = gather_w(1, me_row, x_up, wts)
    w_down = gather_w(2, me_row, x_down, wts)
    cores = [gather_w(7, me_row, core_to, wts)]
    mine = pltpu.make_async_copy(wts, w_at(me_row), local_sem)
    mine.start()
    feat_all[me_col] = feat[...]
    wts_all[no_block] = jnp.zeros_like(wts_all[no_block])

    def w_stage_x():
        w_up.wait_recv()
        slot = row_of(-1, 0, 0)
        first = gather_w(3, slot, x_up)
        cores.append(gather_w(8, slot, core_to))
        w_down.wait_recv()
        cores.append(gather_w(9, row_of(1, 0, 0), core_to))
        w_h.wait_recv()
        slot = row_of(0, 1, 0)
        up = gather_w(4, slot, x_up)
        down = gather_w(5, slot, x_down)
        cores.append(gather_w(10, slot, core_to))
        return first, up, down

    def w_stage_far(first, up, down):
        down.wait_recv()
        slot = row_of(1, 1, 0)
        last = gather_w(6, slot, x_down)
        cores.append(gather_w(11, slot, core_to))
        up.wait_recv()
        cores.append(gather_w(12, row_of(-1, 1, 0), core_to))
        first.wait_recv()
        cores.append(gather_w(13, row_of(2, 0, 0), core_to))
        return last

    def w_stage_last(last):
        last.wait_recv()
        cores.append(gather_w(14, row_of(2, 1, 0), core_to))

    def find_blocks(b, carry):
        for f in range(columns):
            found = jnp.int32(no_block)
            for s in range(slots):
                found = jnp.where(rows[f, s] == b, jnp.int32(f * slots + s), found)
            places_of[b, f] = found
        return carry

    third = Y * Z // 4
    for j in (1, 3, 2):
        yc[j].wait_recv()
        for way in (PLUS, MINUS):
            zc[way, 1, j] = gather_z(way, 1, j)
    pending = None
    for k in range(2, HALF_RING + 1):
        for j in (0, 1, 3, 2):
            for way in (PLUS, MINUS):
                zc[way, k - 1, j].wait_recv()
                zc[way, k, j] = gather_z(way, k, j)
        if k == 2:
            pending = w_stage_x()
        elif k == 3:
            pending = w_stage_far(*pending)
        elif k == 4:
            w_stage_last(pending)
        if k < HALF_RING:
            lax.fori_loop((k - 2) * third, (k - 1) * third, find_blocks, 0)
    mine.wait()
    for copy in cores:
        copy.wait_recv()
    for j in range(Y):
        for way in (PLUS, MINUS):
            zc[way, HALF_RING, j].wait_recv()

    def pick(f):
        return jnp.concatenate([feat_all[rows[f, s]] for s in range(slots)], axis=0)

    c = math.sqrt(2.0 / math.pi)
    for f in range(columns):
        w = wts_all[f * slots : (f + 1) * slots].reshape(slots * 128, 128)
        v = lax.dot_general(w, pick(f), (((0,), (0,)), ((), ())), preferred_element_type=f32)
        sq = v * v
        t = jnp.tanh(c * (v + 0.044715 * (sq * v)))
        gate = 0.5 * (1.0 + t)
        here = pl.ds(f * 128, 128)
        hidden[here, :] = (v * gate).astype(bf16)
        slope = gate + 0.5 * v * (1.0 - t * t) * (c * (1.0 + (3 * 0.044715) * sq))
        grad[here, :] = (upper[here, :].astype(f32) * slope).astype(bf16)

    order = (2, 1, 3, 0)

    def terms(i, dz):
        left = []
        for j in order:
            b = col_of(j, dz)
            left.append(
                jnp.concatenate([wts_all[places_of[b, f]] for f in range(columns)], axis=1)
            )
        term[i] = jnp.dot(jnp.concatenate(left, axis=0), grad[...], preferred_element_type=f32)

    def term_of(i, j, start=0, size=128):
        return term[i, pl.ds(order.index(j) * 128 + start, size), :]

    def send_z(way, k, j):
        step = 1 if way == PLUS else -1
        src, dst = zbuf_s.at[way, k, j], zbuf_r.at[way, k, j]
        if k == 0:
            part = pl.ds(0, half) if way == PLUS else pl.ds(half, half)
            src, dst = src.at[part], dst.at[part]
        return send(src, dst, zs.at[way, k, j], zr.at[way, k, j], col=col_of(0, step))

    def send_x(i, to):
        return send(xbuf_s.at[i], xbuf_r.at[i], xs.at[i], xr.at[i], row=to)

    zc = {}
    terms(PLUS, HALF_RING)
    for j in order:
        for way in (PLUS, MINUS):
            first = 0 if way == PLUS else half
            zbuf_s[way, 0, j, pl.ds(first, half), :] = term_of(PLUS, j, first, half).astype(bf16)
            zc[way, 0, j] = send_z(way, 0, j)

    for f in range(columns):
        wg = lax.dot_general(
            pick(f), grad[pl.ds(f * 128, 128), :], (((1,), (1,)), ((), ())),
            preferred_element_type=f32,
        )
        for s in range(slots):
            w_part[:, pl.ds((f * slots + s) * 8, 8), :] = wg[s * 128 : (s + 1) * 128].reshape(
                X * 4, 8, 128
            )

    dests = [(2, 0), (2, 1), (1, 0), (1, 1), (-1, 0), (-1, 1), (0, 1), (0, 0)]
    cc = []
    for i, (dx, dh) in enumerate(dests):
        cbuf_s[i] = w_part[row_of(dx, dh, 1)].astype(bf16)
        cc.append(send(cbuf_s.at[i], cbuf_r.at[i], cs.at[i], cr.at[i], row=core_to))

    def pair(i):
        dx, dh = dests[i]
        cc[i].wait_recv()
        return w_part[row_of(dx, dh, 0)] + cbuf_r[i].astype(f32)

    xc = {}

    def w_far():
        xbuf_s[0] = pair(0).astype(bf16)
        xc[0] = send_x(0, x_up)
        xbuf_s[1] = pair(1).astype(bf16)
        xc[1] = send_x(1, x_down)
        xbuf_s[2] = pair(3).astype(bf16)
        xc[2] = send_x(2, x_up)
        xbuf_s[3] = pair(4).astype(bf16)
        xc[3] = send_x(3, x_down)

    def w_near():
        xc[0].wait_recv()
        xbuf_s[4] = (pair(2) + xbuf_r[0].astype(f32)).astype(bf16)
        xc[4] = send_x(4, x_up)
        xc[1].wait_recv()
        xbuf_s[5] = (pair(5) + xbuf_r[1].astype(f32)).astype(bf16)
        xc[5] = send_x(5, x_down)
        own[...] = pair(7)

    def w_across():
        xc[2].wait_recv()
        xc[5].wait_recv()
        total = pair(6) + xbuf_r[2].astype(f32) + xbuf_r[5].astype(f32)
        xbuf_s[6] = total.astype(bf16)
        xc[6] = send_x(6, h_to)

    def w_end():
        xc[3].wait_recv()
        xc[4].wait_recv()
        xc[6].wait_recv()
        total = own[...] + xbuf_r[3].astype(f32) + xbuf_r[4].astype(f32) + xbuf_r[6].astype(f32)
        w_out[...] = total * scale

    def add_z(way, k, j):
        zc[way, k - 1, j].wait_recv()
        if k > 1:
            zbuf_s[way, k, j] = (
                term_of(way, j) + zbuf_r[way, k - 1, j].astype(f32)
            ).astype(bf16)
            return
        got, rest = (0, half) if way == PLUS else (half, 0)
        zbuf_s[way, k, j, pl.ds(got, half), :] = (
            term_of(way, j, got, half) + zbuf_r[way, 0, j, pl.ds(got, half), :].astype(f32)
        ).astype(bf16)
        zbuf_s[way, k, j, pl.ds(rest, half), :] = term_of(way, j, rest, half).astype(bf16)

    stages = {1: w_far, 2: w_near, 3: w_across, 4: w_end}
    for k in range(1, HALF_RING):
        terms(PLUS, HALF_RING - k)
        terms(MINUS, k - HALF_RING)
        for j in order:
            for way in (PLUS, MINUS):
                add_z(way, k, j)
                zc[way, k, j] = send_z(way, k, j)
        if k in stages:
            stages[k]()
    terms(PLUS, 0)

    def total_z(j):
        for way in (PLUS, MINUS):
            zc[way, HALF_RING - 1, j].wait_recv()
        return (
            term_of(PLUS, j)
            + zbuf_r[PLUS, HALF_RING - 1, j].astype(f32)
            + zbuf_r[MINUS, HALF_RING - 1, j].astype(f32)
        )

    yc = []
    for j in (2, 1, 3):
        ybuf_s[j - 1] = total_z(j).astype(bf16)
        yc.append(
            send(ybuf_s.at[j - 1], ybuf_r.at[j - 1], ys.at[j - 1], yr.at[j - 1], col=col_of(j, 0))
        )
    total = total_z(0)
    for copy in yc:
        copy.wait_recv()
    for j in range(Y - 1):
        total = total + ybuf_r[j].astype(f32)
    in_out[...] = total.astype(bf16)
    for copy in started:
        copy.wait_send()


def step(rows, features, weights, upper, scale):
    dma = pltpu.SemaphoreType.DMA
    bf16, f32 = jnp.bfloat16, jnp.float32
    block = features.shape
    pieces, side, n = weights.shape
    columns = rows.shape[0]
    piece = (pieces * side, n)
    ring = (2, HALF_RING, Y)
    vmem = pl.BlockSpec(memory_space=VMEM)
    return pl.pallas_call(
        functools.partial(step_kernel, scale),
        out_shape=(
            jax.ShapeDtypeStruct(upper.shape, bf16),
            jax.ShapeDtypeStruct(block, bf16),
            jax.ShapeDtypeStruct(piece, f32),
        ),
        in_specs=[pl.BlockSpec(memory_space=pltpu.SMEM), vmem, vmem, vmem],
        out_specs=(vmem,) * 3,
        scratch_shapes=[
            VMEM((Y * Z,) + block, bf16),
            VMEM((pieces + 1, X * 4 * side, n), bf16),
            pltpu.SMEM((Y * Z, columns), jnp.int32),
            VMEM(upper.shape, bf16),
            VMEM((2, Y * block[0], block[1]), f32),
            VMEM((X * 4,) + piece, f32),
            VMEM(ring + block, bf16), VMEM(ring + block, bf16),
            VMEM((Y - 1,) + block, bf16), VMEM((Y - 1,) + block, bf16),
            VMEM((8,) + piece, bf16), VMEM((8,) + piece, bf16),
            VMEM(piece, f32),
            VMEM((7,) + piece, bf16), VMEM((7,) + piece, bf16),
            dma((Y - 1,)), dma((Y - 1,)),
            dma(ring), dma(ring),
            dma((15,)), dma((15,)),
            dma,
            dma(ring), dma(ring),
            dma((Y - 1,)), dma((Y - 1,)),
            dma((8,)), dma((8,)),
            dma((7,)), dma((7,)),
        ],
        compiler_params=pltpu.CompilerParams(collective_id=1, has_side_effects=True),
        name="layer_and_gradients",
    )(rows, features, weights, upper)


def finish_kernel(hidden, in_grad, w_grad, hidden_out, in_out, w_out):
    hidden_out[...] = hidden[...]
    in_out[...] = in_grad[...]
    w_out[...] = w_grad[...]


def finish(*arrays):
    return pl.pallas_call(
        finish_kernel,
        out_shape=tuple(jax.ShapeDtypeStruct(a.shape, a.dtype) for a in arrays),
        in_specs=[pl.BlockSpec(memory_space=VMEM)] * 3,
        out_specs=(pl.BlockSpec(memory_space=VMEM),) * 3,
        name="outputs",
    )(*arrays)


def local(features, weight_blocks, block_rows, upstream):
    grad_scale = float(features.shape[1] * lax.axis_size("row")) ** (-0.5)
    weights = weight_blocks.reshape((-1,) + weight_blocks.shape[2:])
    hidden, input_grad, w_grad = finish(
        *step(block_rows, features, weights, upstream, grad_scale)
    )
    return (hidden, input_grad, w_grad.reshape(weight_blocks.shape))


def solution(mesh):
    return jax.shard_map(
        local,
        mesh=mesh,
        in_specs=(P("col", "row"), P("col", None, "row", None), P("col", None), P("col", "row")),
        out_specs=(P("col", "row"), P("col", "row"), P("col", None, "row", None)),
        check_vma=False,
    )
```

time: 124 us -> 101 us (0.81)
  Pallas kernels: 116 us -> 99.8 us
  local copies, waits for them, and re-layouts: 6.15 us -> 0 us
    pallas_call x3 -> x2, Pallas kernels: 116 us -> 99.8 us  [the longest x1 97.8 us: step(): pl.pallas_call(functools.partial(step_kernel, scale), out_shape=(jax.Shap...]
    unnamed x2 -> x0, local copies, waits for them, and re-layouts: 3.09 us -> none
    reshape x1 -> x0, local copies, waits for them, and re-layouts: 3.06 us -> none  [local(): pieces.reshape(-1, cols, slots, rows_here, n).transpose(1, 2, 0, 3, 4)]
where the time goes in v2:
time: 101 us; the launch traced here: 100 us
  Pallas kernels  99.8 us (99%)
    pallas_call x1, Pallas kernels, step(): pl.pallas_call(functools.partial(step_kernel, scale), out_shape=(jax.Shap...  97.8 us

profile of v2, /device:TPU:6, one launch (start us, length us, event | category | flops | bytes accessed | tf_op | source)
XLA Modules:
  0.0 100.4 jit_solution(3818857912557612870)
XLA Ops:
  0.6 97.8 %layer_and_gradients.1 = (bf16[1024,256]{1,0:T(8,128)(2,1)}, bf16[128,256]{1,0:T(8,128)(2,1)}, f32[384,128]{1,0:T(8,128)}) custom-call(s32[8,6]{1,0:T(8,128)} %rows.1, bf16[128,256]{1,0:T(8,128)(2,1)} %feat.1, bf16[48,8,128]{2,1,0:T(8,128)(2,1)} %bitcast.2, bf16[1024,256]{1,0:T(8,128)(2,1)} %upper.1), custom_call_target="tpu_custom_call" | custom-call | tf_op jit(solution)/shard_map/layer_and_gradients/pallas_call | solution.py:328
  98.4 2.0 %outputs.1 = (bf16[1024,256]{1,0:T(8,128)(2,1)}, bf16[128,256]{1,0:T(8,128)(2,1)}, f32[384,128]{1,0:T(8,128)}) custom-call(bf16[1024,256]{1,0:T(8,128)(2,1)} %get-tuple-element.9.hidden, bf16[128,256]{1,0:T(8,128)(2,1)} %get-tuple-element.10.in_grad, f32[384,128]{1,0:T(8,128)} %get-tuple-element.11.w_grad), custom_call_target="tpu_custom_call" | custom-call | tf_op jit(solution)/shard_map/outputs/pallas_call | solution.py:370

commit v3 on v2

--- a/solution.py
+++ b/solution.py
@@ -12,6 +12,7 @@
 X = 4
 HALF_RING = Z // 2
 PLUS, MINUS = 0, 1
+SPREAD = 32
 VMEM = pltpu.VMEM
 
 
@@ -45,12 +46,14 @@
     scale, rows, feat, wts, upper, hidden, in_out, w_out,
     feat_all, wts_all, places_of, grad, term, w_part,
     zbuf_s, zbuf_r, ybuf_s, ybuf_r, cbuf_s, cbuf_r, own, xbuf_s, xbuf_r,
-    gys, gyr, gzs, gzr, gws, gwr, local_sem,
-    zs, zr, ys, yr, cs, cr, xs, xr,
+    sbuf_s, sbuf_r,
+    gys, gyr, gzs, gzr, gws, gwr, gss, gsr, local_sem,
+    zs, zr, ys, yr, cs, cr, xs, xr, ss, sr,
 ):
     col_of, row_of = places()
     me_col, me_row = col_of(0, 0), row_of(0, 0, 0)
-    half = feat.shape[0] // 2
+    whole = feat.shape[0]
+    ringed = whole - SPREAD
     f32, bf16 = jnp.float32, jnp.bfloat16
     columns, slots = rows.shape
     no_block = columns * slots
@@ -63,6 +66,16 @@
         copy.start()
         started.append(copy)
         return copy
+
+    def height(j):
+        return whole if j == 0 else ringed
+
+    def share(way, j):
+        cut = min(whole // 2, height(j) - height(j) // 32 * 16)
+        return (0, cut) if way == PLUS else (cut, height(j) - cut)
+
+    def index_of(way, k):
+        return 10 if k == HALF_RING else way * 5 + k - 1
 
     def w_at(slot):
         return wts_all.at[pl.ds(0, no_block), pl.ds(pl.multiple_of(slot * 8, 8), 8), :]
@@ -75,8 +88,8 @@
         slot = col_of(j, -step * (k - 1))
         src = feat if (j == 0 and k == 1) else feat_all.at[slot]
         dst = feat_all.at[slot]
-        if k == HALF_RING:
-            part = pl.ds(0, half) if way == PLUS else pl.ds(half, half)
+        if k == HALF_RING or j != 0:
+            part = pl.ds(*(share(way, j) if k == HALF_RING else (0, ringed)))
             src, dst = src.at[part], dst.at[part]
         return send(src, dst, gzs.at[way, k - 1, j], gzr.at[way, k - 1, j], col=col_of(0, step))
 
@@ -90,7 +103,6 @@
         zc[way, 1, 0] = gather_z(way, 1, 0)
     for j in (1, 3, 2):
         yc[j] = send(feat, feat_all.at[me_col], gys.at[j - 1], gyr.at[j - 1], col=col_of(4 - j, 0))
-    w_h = gather_w(0, me_row, h_to, wts)
     w_up = gather_w(1, me_row, x_up, wts)
     w_down = gather_w(2, me_row, x_down, wts)
     cores = [gather_w(7, me_row, core_to, wts)]
@@ -99,33 +111,36 @@
     feat_all[me_col] = feat[...]
     wts_all[no_block] = jnp.zeros_like(wts_all[no_block])
 
+    w_h = None
+    wc = {}
+
     def w_stage_x():
         w_up.wait_recv()
         slot = row_of(-1, 0, 0)
-        first = gather_w(3, slot, x_up)
+        wc["first"] = gather_w(3, slot, x_up)
         cores.append(gather_w(8, slot, core_to))
         w_down.wait_recv()
         cores.append(gather_w(9, row_of(1, 0, 0), core_to))
+
+    def w_stage_h():
         w_h.wait_recv()
         slot = row_of(0, 1, 0)
-        up = gather_w(4, slot, x_up)
-        down = gather_w(5, slot, x_down)
+        wc["up"] = gather_w(4, slot, x_up)
+        wc["down"] = gather_w(5, slot, x_down)
         cores.append(gather_w(10, slot, core_to))
-        return first, up, down
-
-    def w_stage_far(first, up, down):
-        down.wait_recv()
+        wc["first"].wait_recv()
+        cores.append(gather_w(13, row_of(2, 0, 0), core_to))
+
+    def w_stage_far():
+        wc["down"].wait_recv()
         slot = row_of(1, 1, 0)
-        last = gather_w(6, slot, x_down)
+        wc["last"] = gather_w(6, slot, x_down)
         cores.append(gather_w(11, slot, core_to))
-        up.wait_recv()
+        wc["up"].wait_recv()
         cores.append(gather_w(12, row_of(-1, 1, 0), core_to))
-        first.wait_recv()
-        cores.append(gather_w(13, row_of(2, 0, 0), core_to))
-        return last
-
-    def w_stage_last(last):
-        last.wait_recv()
+
+    def w_stage_last():
+        wc["last"].wait_recv()
         cores.append(gather_w(14, row_of(2, 1, 0), core_to))
 
     def find_blocks(b, carry):
@@ -136,31 +151,54 @@
             places_of[b, f] = found
         return carry
 
-    third = Y * Z // 4
-    for j in (1, 3, 2):
+    quarter = Y * Z // 4
+    spread = []
+
+    def spread_y(way, k):
+        slot = col_of(0, -k if way == PLUS else k)
+        part = feat_all.at[slot].at[pl.ds(ringed, SPREAD)]
+        i = index_of(way, k)
+        for d in (1, 3, 2):
+            spread.append(
+                send(part, part, gss.at[i, d - 1], gsr.at[i, d - 1], col=col_of(d, 0))
+            )
+
+    def pass_on(k, j):
+        for way in (PLUS, MINUS):
+            zc[way, k, j].wait_recv()
+            if k < HALF_RING:
+                zc[way, k + 1, j] = gather_z(way, k + 1, j)
+            if j == 0 and (k < HALF_RING or way == MINUS):
+                spread_y(way, k)
+
+    def begin(j):
         yc[j].wait_recv()
         for way in (PLUS, MINUS):
             zc[way, 1, j] = gather_z(way, 1, j)
-    pending = None
-    for k in range(2, HALF_RING + 1):
-        for j in (0, 1, 3, 2):
-            for way in (PLUS, MINUS):
-                zc[way, k - 1, j].wait_recv()
-                zc[way, k, j] = gather_z(way, k, j)
-        if k == 2:
-            pending = w_stage_x()
-        elif k == 3:
-            pending = w_stage_far(*pending)
-        elif k == 4:
-            w_stage_last(pending)
-        if k < HALF_RING:
-            lax.fori_loop((k - 2) * third, (k - 1) * third, find_blocks, 0)
+
+    pass_on(1, 0)
+    begin(1)
+    begin(3)
+    pass_on(2, 0)
+    begin(2)
+    w_h = gather_w(0, me_row, h_to, wts)
+    stages = {1: w_stage_x, 2: w_stage_h, 3: w_stage_far, 4: w_stage_last}
+    for k in range(1, HALF_RING):
+        if k + 2 <= HALF_RING:
+            pass_on(k + 2, 0)
+        for j in (1, 3, 2):
+            pass_on(k, j)
+        if k in stages:
+            stages[k]()
+            lax.fori_loop((k - 1) * quarter, k * quarter, find_blocks, 0)
     mine.wait()
     for copy in cores:
         copy.wait_recv()
-    for j in range(Y):
+    for j in range(1, Y):
         for way in (PLUS, MINUS):
             zc[way, HALF_RING, j].wait_recv()
+    for copy in spread:
+        copy.wait_recv()
 
     def pick(f):
         return jnp.concatenate([feat_all[rows[f, s]] for s in range(slots)], axis=0)
@@ -178,37 +216,75 @@
         grad[here, :] = (upper[here, :].astype(f32) * slope).astype(bf16)
 
     order = (2, 1, 3, 0)
-
-    def terms(i, dz):
+    others = order[:-1]
+
+    def terms(way, k, dz):
         left = []
         for j in order:
             b = col_of(j, dz)
             left.append(
                 jnp.concatenate([wts_all[places_of[b, f]] for f in range(columns)], axis=1)
             )
-        term[i] = jnp.dot(jnp.concatenate(left, axis=0), grad[...], preferred_element_type=f32)
-
-    def term_of(i, j, start=0, size=128):
-        return term[i, pl.ds(order.index(j) * 128 + start, size), :]
+        term[way, k % 2] = jnp.dot(jnp.concatenate(left, axis=0), grad[...], preferred_element_type=f32)
+
+    def term_of(way, k, j, start=0, size=128):
+        return term[way, k % 2, pl.ds(order.index(j) * 128 + start, size), :]
 
     def send_z(way, k, j):
         step = 1 if way == PLUS else -1
-        src, dst = zbuf_s.at[way, k, j], zbuf_r.at[way, k, j]
-        if k == 0:
-            part = pl.ds(0, half) if way == PLUS else pl.ds(half, half)
-            src, dst = src.at[part], dst.at[part]
-        return send(src, dst, zs.at[way, k, j], zr.at[way, k, j], col=col_of(0, step))
+        part = pl.ds(*(share(way, j) if k == 0 else (0, height(j))))
+        return send(
+            zbuf_s.at[way, k, j, part], zbuf_r.at[way, k, j, part],
+            zs.at[way, k, j], zr.at[way, k, j], col=col_of(0, step),
+        )
 
     def send_x(i, to):
         return send(xbuf_s.at[i], xbuf_r.at[i], xs.at[i], xr.at[i], row=to)
 
     zc = {}
-    terms(PLUS, HALF_RING)
-    for j in order:
-        for way in (PLUS, MINUS):
-            first = 0 if way == PLUS else half
-            zbuf_s[way, 0, j, pl.ds(first, half), :] = term_of(PLUS, j, first, half).astype(bf16)
+    sc = {}
+
+    def send_spread(way, k):
+        i = index_of(way, HALF_RING - k)
+        for j in others:
+            sbuf_s[i, j - 1] = term_of(way, k, j, ringed, SPREAD).astype(bf16)
+            sc[i, j] = send(
+                sbuf_s.at[i, j - 1], sbuf_r.at[i, j - 1],
+                ss.at[i, j - 1], sr.at[i, j - 1], col=col_of(j, 0),
+            )
+
+    def own_term(way, k, start, size):
+        value = term_of(way, k, 0, start, size)
+        if start + size < whole:
+            return [(start, size, value)]
+        i = index_of(way, HALF_RING - k)
+        for j in others:
+            sc[i, j].wait_recv()
+        last = value[ringed - start :]
+        for j in others:
+            last = last + sbuf_r[i, j - 1].astype(f32)
+        return [(start, ringed - start, value[: ringed - start]), (ringed, SPREAD, last)]
+
+    def put(way, k, j, source, start, size, arrived):
+        pieces = (
+            own_term(source, k, start, size)
+            if j == 0
+            else [(start, size, term_of(source, k, j, start, size))]
+        )
+        for at, n, value in pieces:
+            if arrived:
+                value = value + zbuf_r[way, k - 1, j, pl.ds(at, n), :].astype(f32)
+            zbuf_s[way, k, j, pl.ds(at, n), :] = value.astype(bf16)
+
+    def first_z(j):
+        for way in (PLUS, MINUS):
+            put(way, 0, j, PLUS, *share(way, j), False)
             zc[way, 0, j] = send_z(way, 0, j)
+
+    terms(PLUS, 0, HALF_RING)
+    for j in others:
+        first_z(j)
+    send_spread(PLUS, 0)
 
     for f in range(columns):
         wg = lax.dot_general(
@@ -266,43 +342,52 @@
         total = own[...] + xbuf_r[3].astype(f32) + xbuf_r[4].astype(f32) + xbuf_r[6].astype(f32)
         w_out[...] = total * scale
 
-    def add_z(way, k, j):
-        zc[way, k - 1, j].wait_recv()
-        if k > 1:
-            zbuf_s[way, k, j] = (
-                term_of(way, j) + zbuf_r[way, k - 1, j].astype(f32)
-            ).astype(bf16)
-            return
-        got, rest = (0, half) if way == PLUS else (half, 0)
-        zbuf_s[way, k, j, pl.ds(got, half), :] = (
-            term_of(way, j, got, half) + zbuf_r[way, 0, j, pl.ds(got, half), :].astype(f32)
-        ).astype(bf16)
-        zbuf_s[way, k, j, pl.ds(rest, half), :] = term_of(way, j, rest, half).astype(bf16)
+    def add_z(k, j):
+        for way in (PLUS, MINUS):
+            zc[way, k - 1, j].wait_recv()
+            if k > 1:
+                put(way, k, j, way, 0, height(j), True)
+            elif way == PLUS:
+                put(way, k, j, way, *share(PLUS, j), True)
+                put(way, k, j, way, *share(MINUS, j), False)
+            else:
+                put(way, k, j, way, *share(PLUS, j), False)
+                put(way, k, j, way, *share(MINUS, j), True)
+            zc[way, k, j] = send_z(way, k, j)
 
     stages = {1: w_far, 2: w_near, 3: w_across, 4: w_end}
     for k in range(1, HALF_RING):
-        terms(PLUS, HALF_RING - k)
-        terms(MINUS, k - HALF_RING)
-        for j in order:
-            for way in (PLUS, MINUS):
-                add_z(way, k, j)
-                zc[way, k, j] = send_z(way, k, j)
+        terms(PLUS, k, HALF_RING - k)
+        terms(MINUS, k, k - HALF_RING)
+        send_spread(PLUS, k)
+        send_spread(MINUS, k)
+        for j in others:
+            add_z(k, j)
+        if k == 1:
+            first_z(0)
+        else:
+            add_z(k - 1, 0)
         if k in stages:
             stages[k]()
-    terms(PLUS, 0)
+    last = HALF_RING - 1
+    terms(PLUS, last + 1, 0)
+    add_z(last, 0)
 
     def total_z(j):
         for way in (PLUS, MINUS):
-            zc[way, HALF_RING - 1, j].wait_recv()
+            zc[way, last, j].wait_recv()
         return (
-            term_of(PLUS, j)
-            + zbuf_r[PLUS, HALF_RING - 1, j].astype(f32)
-            + zbuf_r[MINUS, HALF_RING - 1, j].astype(f32)
+            term_of(PLUS, last + 1, j, 0, height(j))
+            + zbuf_r[PLUS, last, j, pl.ds(0, height(j)), :].astype(f32)
+            + zbuf_r[MINUS, last, j, pl.ds(0, height(j)), :].astype(f32)
         )
 
     yc = []
     for j in (2, 1, 3):
-        ybuf_s[j - 1] = total_z(j).astype(bf16)
+        ybuf_s[j - 1, pl.ds(0, ringed), :] = total_z(j).astype(bf16)
+        ybuf_s[j - 1, pl.ds(ringed, SPREAD), :] = term_of(
+            PLUS, last + 1, j, ringed, SPREAD
+        ).astype(bf16)
         yc.append(
             send(ybuf_s.at[j - 1], ybuf_r.at[j - 1], ys.at[j - 1], yr.at[j - 1], col=col_of(j, 0))
         )
@@ -324,6 +409,7 @@
     columns = rows.shape[0]
     piece = (pieces * side, n)
     ring = (2, HALF_RING, Y)
+    spread = (Z - 1, Y - 1, SPREAD, block[1])
     vmem = pl.BlockSpec(memory_space=VMEM)
     return pl.pallas_call(
         functools.partial(step_kernel, scale),
@@ -339,21 +425,24 @@
             VMEM((pieces + 1, X * 4 * side, n), bf16),
             pltpu.SMEM((Y * Z, columns), jnp.int32),
             VMEM(upper.shape, bf16),
-            VMEM((2, Y * block[0], block[1]), f32),
+            VMEM((2, 2, Y * block[0], block[1]), f32),
             VMEM((X * 4,) + piece, f32),
             VMEM(ring + block, bf16), VMEM(ring + block, bf16),
             VMEM((Y - 1,) + block, bf16), VMEM((Y - 1,) + block, bf16),
             VMEM((8,) + piece, bf16), VMEM((8,) + piece, bf16),
             VMEM(piece, f32),
             VMEM((7,) + piece, bf16), VMEM((7,) + piece, bf16),
+            VMEM(spread, bf16), VMEM(spread, bf16),
             dma((Y - 1,)), dma((Y - 1,)),
             dma(ring), dma(ring),
             dma((15,)), dma((15,)),
+            dma(spread[:2]), dma(spread[:2]),
             dma,
             dma(ring), dma(ring),
             dma((Y - 1,)), dma((Y - 1,)),
             dma((8,)), dma((8,)),
             dma((7,)), dma((7,)),
+            dma(spread[:2]), dma(spread[:2]),
         ],
         compiler_params=pltpu.CompilerParams(collective_id=1, has_side_effects=True),
         name="layer_and_gradients",

time: 101 us -> 95.8 us (0.949)
  Pallas kernels: 99.8 us -> 94.1 us
    pallas_call x1, Pallas kernels: 97.8 us -> 92.1 us  [step(): pl.pallas_call(functools.partial(step_kernel, scale), out_shape=(jax.Shap...]
where the time goes in v3:
time: 95.8 us; the launch traced here: 94.8 us
  Pallas kernels  94.1 us (98%)
    pallas_call x1, Pallas kernels, step(): pl.pallas_call(functools.partial(step_kernel, scale), out_shape=(jax.Shap...  92.1 us
    pallas_call x1, Pallas kernels, finish(): pl.pallas_call(finish_kernel, out_shape=tuple((jax.ShapeDtypeStruct(a.sha...  2.01 us

profile of v3, /device:TPU:6, one launch (start us, length us, event | category | flops | bytes accessed | tf_op | source)
XLA Modules:
  0.0 94.8 jit_solution(12968216597375774495)
XLA Ops:
  0.6 92.1 %layer_and_gradients.1 = (bf16[1024,256]{1,0:T(8,128)(2,1)}, bf16[128,256]{1,0:T(8,128)(2,1)}, f32[384,128]{1,0:T(8,128)}) custom-call(s32[8,6]{1,0:T(8,128)} %rows.1, bf16[128,256]{1,0:T(8,128)(2,1)} %feat.1, bf16[48,8,128]{2,1,0:T(8,128)(2,1)} %bitcast.2, bf16[1024,256]{1,0:T(8,128)(2,1)} %upper.1), custom_call_target="tpu_custom_call" | custom-call | tf_op jit(solution)/shard_map/layer_and_gradients/pallas_call | solution.py:414
  92.8 2.0 %outputs.1 = (bf16[1024,256]{1,0:T(8,128)(2,1)}, bf16[128,256]{1,0:T(8,128)(2,1)}, f32[384,128]{1,0:T(8,128)}) custom-call(bf16[1024,256]{1,0:T(8,128)(2,1)} %get-tuple-element.9.hidden, bf16[128,256]{1,0:T(8,128)(2,1)} %get-tuple-element.10.in_grad, f32[384,128]{1,0:T(8,128)} %get-tuple-element.11.w_grad), custom_call_target="tpu_custom_call" | custom-call | tf_op jit(solution)/shard_map/outputs/pallas_call | solution.py:459

commit v4 on v3

--- a/solution.py
+++ b/solution.py
@@ -168,8 +168,12 @@
             zc[way, k, j].wait_recv()
             if k < HALF_RING:
                 zc[way, k + 1, j] = gather_z(way, k + 1, j)
-            if j == 0 and (k < HALF_RING or way == MINUS):
-                spread_y(way, k)
+        if j == 0 and k > 2:
+            spread_both(k)
+
+    def spread_both(k):
+        for way in (PLUS, MINUS) if k < HALF_RING else (MINUS,):
+            spread_y(way, k)
 
     def begin(j):
         yc[j].wait_recv()
@@ -181,6 +185,8 @@
     begin(3)
     pass_on(2, 0)
     begin(2)
+    spread_both(1)
+    spread_both(2)
     w_h = gather_w(0, me_row, h_to, wts)
     stages = {1: w_stage_x, 2: w_stage_h, 3: w_stage_far, 4: w_stage_last}
     for k in range(1, HALF_RING):

time: 95.8 us -> 93.7 us (0.978)
  Pallas kernels: 94.1 us -> 92.9 us
    pallas_call x1, Pallas kernels: 92.1 us -> 90.9 us  [step(): pl.pallas_call(functools.partial(step_kernel, scale), out_shape=(jax.Shap...]
where the time goes in v4:
time: 93.7 us; the launch traced here: 93.6 us
  Pallas kernels  92.9 us (99%)
    pallas_call x1, Pallas kernels, step(): pl.pallas_call(functools.partial(step_kernel, scale), out_shape=(jax.Shap...  90.9 us
    pallas_call x1, Pallas kernels, finish(): pl.pallas_call(finish_kernel, out_shape=tuple((jax.ShapeDtypeStruct(a.sha...  2.01 us

profile of v4, /device:TPU:6, one launch (start us, length us, event | category | flops | bytes accessed | tf_op | source)
XLA Modules:
  0.0 93.6 jit_solution(6006417072924868465)
XLA Ops:
  0.6 90.9 %layer_and_gradients.1 = (bf16[1024,256]{1,0:T(8,128)(2,1)}, bf16[128,256]{1,0:T(8,128)(2,1)}, f32[384,128]{1,0:T(8,128)}) custom-call(s32[8,6]{1,0:T(8,128)} %rows.1, bf16[128,256]{1,0:T(8,128)(2,1)} %feat.1, bf16[48,8,128]{2,1,0:T(8,128)(2,1)} %bitcast.2, bf16[1024,256]{1,0:T(8,128)(2,1)} %upper.1), custom_call_target="tpu_custom_call" | custom-call | tf_op jit(solution)/shard_map/layer_and_gradients/pallas_call | solution.py:420
  91.6 2.0 %outputs.1 = (bf16[1024,256]{1,0:T(8,128)(2,1)}, bf16[128,256]{1,0:T(8,128)(2,1)}, f32[384,128]{1,0:T(8,128)}) custom-call(bf16[1024,256]{1,0:T(8,128)(2,1)} %get-tuple-element.9.hidden, bf16[128,256]{1,0:T(8,128)(2,1)} %get-tuple-element.10.in_grad, f32[384,128]{1,0:T(8,128)} %get-tuple-element.11.w_grad), custom_call_target="tpu_custom_call" | custom-call | tf_op jit(solution)/shard_map/outputs/pallas_call | solution.py:465
